TPU v7x, 512 devices: a whole 4x8x8 slice. The times are simulated.
512 devices in a mesh: ctx: 64 (over x, y, core), tp: 8 (over z).
Axes of the slice: x: 4, y: 8, z: 8, core: 2. Of those that a mesh axis runs over, the one named last changes fastest.
Arguments:
- queries: bfloat16 [32768, 2048], P('ctx', 'tp'), may hold values from -1.75 to 1.75
- keys: bfloat16 [32768, 2048], P('ctx', 'tp'), may hold values from -1.75 to 1.75
- values: bfloat16 [32768, 2048], P('ctx', 'tp'), may hold values from -18 to 18
- gain: bfloat16 [2048], P('tp'), may hold values from 0.099609375 to 1.8984375
- cotangent: bfloat16 [32768, 2048], P('ctx', 'tp'), may hold values from -6 to 6
Outputs:
- normed: bfloat16 [32768, 2048], P('ctx', 'tp')
- grad_queries: bfloat16 [32768, 2048], P('ctx', 'tp')
- grad_keys: bfloat16 [32768, 2048], P('ctx', 'tp')
- grad_values: bfloat16 [32768, 2048], P('ctx', 'tp')
All inputs are finite; a program needn't handle non-finite values.
Results may differ from a plain program's by a relative error of at most 0.0058.
Values sent between devices are 32-bit elements; how exact they have to be, the bound alone decides.
A program may use at most 64 MiB of HBM per device.

v0:
```python
import jax
import jax.numpy as jnp
from jax import lax
from jax.sharding import PartitionSpec as P

HEAD = 128
HEADS = 16
epsilon = 1e-06


def heads_first(matrix, head_count):
    return matrix.reshape(matrix.shape[0], head_count, HEAD).transpose(1, 0, 2)


def heads_last(tensor):
    return tensor.transpose(1, 0, 2).reshape(tensor.shape[1], -1)


def shards(queries, keys, values, gain, cotangent):
    row_count = queries.shape[0]
    head_count = queries.shape[1] // HEAD
    query_heads = heads_first(queries, head_count)
    key_heads = heads_first(keys, head_count)
    value_heads = heads_first(values, head_count)
    causal = jnp.tril(jnp.ones((row_count, row_count), jnp.bool_))
    gain_wide = gain.astype(jnp.float32)
    own_state = jnp.einsum(
        "hte,htf->hef", key_heads, value_heads, preferred_element_type=jnp.float32
    )
    position = lax.axis_index("ctx")
    pieces = lax.all_gather(own_state[None], "ctx", axis=0, tiled=True)
    shard_index = jnp.arange(pieces.shape[0], dtype=jnp.int32)
    lower_mask = (shard_index < position).astype(jnp.float32)
    prior_state = jnp.sum(pieces * lower_mask[:, None, None, None], axis=0)
    prior_low = prior_state.astype(jnp.bfloat16)

    def forward_head(members):
        query_now, key_now, value_now, prior_now = members
        scores = jnp.einsum("te,se->ts", query_now, key_now, preferred_element_type=jnp.float32)
        masked = jnp.where(causal, scores, 0.0).astype(jnp.bfloat16)
        combined = jnp.dot(masked, value_now, preferred_element_type=jnp.float32)
        combined = combined + jnp.dot(query_now, prior_now, preferred_element_type=jnp.float32)
        return (masked, combined)

    masked, combined = lax.map(forward_head, (query_heads, key_heads, value_heads, prior_low))
    attended = heads_last(combined)
    scaled = cotangent.astype(jnp.float32) * gain_wide
    totals = lax.psum(
        (jnp.sum(attended * attended, axis=-1), jnp.sum(scaled * attended, axis=-1)), "tp"
    )
    feature_count = HEADS * HEAD
    inverse = lax.rsqrt(totals[0] / feature_count + epsilon)
    mean_product = totals[1] / feature_count
    normed = (attended * inverse[:, None] * gain_wide).astype(jnp.bfloat16)
    grad_att = (
        inverse[:, None] * scaled - (inverse**3 * mean_product)[:, None] * attended
    ).astype(jnp.bfloat16)
    grad_heads = heads_first(grad_att, head_count)

    def middle_head(members):
        query_now, key_now, value_now, grad_now, prior_now = members
        products = jnp.einsum("te,se->ts", grad_now, value_now, preferred_element_type=jnp.float32)
        cross_low = jnp.where(causal, products, 0.0).astype(jnp.bfloat16)
        grad_query = jnp.dot(cross_low, key_now, preferred_element_type=jnp.float32)
        grad_query = grad_query + jnp.einsum(
            "tf,ef->te", grad_now, prior_now, preferred_element_type=jnp.float32
        )
        later_own = jnp.einsum("te,tf->ef", query_now, grad_now, preferred_element_type=jnp.float32)
        return (cross_low, grad_query.astype(jnp.bfloat16), later_own)

    cross_low, grad_query, later_own = lax.map(
        middle_head, (query_heads, key_heads, value_heads, grad_heads, prior_low)
    )
    position_now = lax.axis_index("ctx")
    pieces = lax.all_gather(later_own[None], "ctx", axis=0, tiled=True)
    shard_index = jnp.arange(pieces.shape[0], dtype=jnp.int32)
    upper_mask = (shard_index > position_now).astype(jnp.float32)
    after_state = jnp.sum(pieces * upper_mask[:, None, None, None], axis=0)
    after_low = after_state.astype(jnp.bfloat16)

    def final_head(members):
        query_now, key_now, value_now, grad_now, masked_now, cross_now, after_now = members
        grad_key = jnp.einsum("st,se->te", cross_now, query_now, preferred_element_type=jnp.float32)
        grad_key = grad_key + jnp.einsum(
            "tf,ef->te", value_now, after_now, preferred_element_type=jnp.float32
        )
        grad_value = jnp.einsum(
            "st,sf->tf", masked_now, grad_now, preferred_element_type=jnp.float32
        )
        grad_value = grad_value + jnp.dot(key_now, after_now, preferred_element_type=jnp.float32)
        return (grad_key.astype(jnp.bfloat16), grad_value.astype(jnp.bfloat16))

    grad_key, grad_value = lax.map(
        final_head, (query_heads, key_heads, value_heads, grad_heads, masked, cross_low, after_low)
    )
    return (normed, heads_last(grad_query), heads_last(grad_key), heads_last(grad_value))


def solution(mesh):
    in_specs = (P("ctx", "tp"), P("ctx", "tp"), P("ctx", "tp"), P("tp"), P("ctx", "tp"))
    out_specs = (P("ctx", "tp"), P("ctx", "tp"), P("ctx", "tp"), P("ctx", "tp"))
    return jax.shard_map(shards, mesh=mesh, in_specs=in_specs, out_specs=out_specs, check_vma=False)
```

profile of v0, /device:TPU:1, one launch (start us, length us, event | category | flops | bytes accessed | tf_op | source)
XLA Modules:
  0.0 234.4 jit_solution(15956539192981530037)
XLA Ops:
  7.2 0.0 all-gather.5.cloned.1.call-start
  7.2 1.1 copy.34
  8.3 1.1 copy.35
  9.4 0.9 fusion.81
  10.3 0.0 all-gather.7.cloned.1.call-start
  10.4 0.2 copy.38
  10.5 0.2 copy.39
  10.8 1.1 copy.33
  11.8 0.2 copy.37
  12.0 0.7 convert_element_type.49
  12.7 93.3 %all-gather.5.cloned.1.call-done = f32[128,128,128]{2,1,0:T(8,128)} async-done(((f32[2,128,128]{2,1,0:T(8,128)}), f32[128,128,128]{2,1,0:T(8,128)}) %all-gather.5.cloned.1.call-update) | async-done | bytes 8388624 | tf_op jit(solution)/shard_map/all_gather | solution.py:31
  106.0 4.1 %multiply_reduce_fusion.1 = bf16[2,128,128]{2,1,0:T(8,128)(2,1)S(1)} fusion(f32[64,2,128,128]{3,2,1,0:T(8,128)} %bitcast.213, f32[64]{0:T(128)S(1)} %compare_convert_fusion.1), kind=kLoop, calls=%fused_computation.83 | loop fusion | flops 4161536 | bytes 8454400 | tf_op jit(solution)/shard_map/reduce_sum | solution.py:34
  110.1 0.1 broadcast.22.clone
  110.2 1.6 while.41
  110.2 0.3 bitcast_dynamic-update-slice_fusion.4
  110.5 0.3 fusion.134
  110.8 0.2 fusion.135
  111.0 0.3 bitcast_dynamic-update-slice_fusion.4
  111.3 0.3 fusion.134
  111.6 0.2 fusion.135
  111.8 0.1 fusion.78
  112.0 0.1 fusion.75
  112.2 14.4 %all-reduce = (f32[512]{0:T(512)S(1)}, f32[512]{0:T(512)S(1)}) all-reduce(f32[512]{0:T(512)S(1)} %fusion.78, f32[512]{0:T(512)S(1)} %fusion.75), channel_id=1, replica_groups=mesh['ctx'=64,'tp'=8] {'tp'}, use_global_device_ids=true, to_apply=%region_4.5 | all-reduce | flops 1024 | bytes 8192 | tf_op jit(solution)/shard_map/psum | solution.py:48
  126.6 0.9 fusion.79
  127.5 0.1 broadcast.22
  127.6 3.4 %while.42 = (s32[]{:T(128)}, bf16[2,512,512]{2,1,0:T(8,128)(2,1)S(1)}, bf16[2,512,128]{2,1,0:T(8,128)(2,1)S(1)}, f32[2,128,128]{2,1,0:T(8,128)}, bf16[2,512,128]...) while((s32[]{:T(128)}, ...), condition=%wide.region_8.9_spmd.clone, body=%wide.region_7.8_spmd.clone.sunk | while | flops 168689664 | bytes 3117673 | solution.py:71
  127.6 0.3 bitcast_dynamic-update-slice_fusion.5
  128.0 0.3 fusion.142
  128.3 0.2 fusion.143
  128.5 0.9 fusion.144
  129.3 0.3 bitcast_dynamic-update-slice_fusion.5
  129.7 0.3 fusion.142
  130.0 0.2 fusion.143
  130.2 0.9 fusion.144
  131.1 0.7 copy_bitcast_fusion.2
  131.8 85.6 %all-gather.7.cloned.1.call-done = f32[128,128,128]{2,1,0:T(8,128)} async-done(((f32[2,128,128]{2,1,0:T(8,128)}), f32[128,128,128]{2,1,0:T(8,128)}) %all-gather.7.cloned.1.call-update) | async-done | bytes 8388624 | tf_op jit(solution)/shard_map/all_gather | solution.py:75
  217.5 4.1 %multiply_reduce_fusion = bf16[2,128,128]{2,1,0:T(8,128)(2,1)S(1)} fusion(f32[64,2,128,128]{3,2,1,0:T(8,128)} %bitcast.214, f32[64]{0:T(128)S(1)} %compare_convert_fusion), kind=kLoop, calls=%fused_computation.82 | loop fusion | flops 4161536 | bytes 8454400 | tf_op jit(solution)/shard_map/reduce_sum | solution.py:78
  221.6 0.7 broadcast.24.clone.1
  222.3 3.4 %while.40 = (s32[]{:T(128)}, bf16[2,512,128]{2,1,0:T(8,128)(2,1)S(1)}, bf16[2,512,128]{2,1,0:T(8,128)(2,1)}, bf16[2,512,512]{2,1,0:T(8,128)(2,1)S(1)}, bf16[2,51...) while((s32[]{:T(128)}, ...), condition=%wide.region_11.12_spmd, body=%wide.region_10.11_spmd.sunk | while | flops 168034304 | bytes 2954349 | solution.py:93
  222.3 0.3 fusion.126
  222.7 0.2 fusion.127
  222.9 0.3 fusion.128
  223.2 0.8 fusion.129
  224.1 0.3 fusion.126
  224.4 0.2 fusion.127
  224.6 0.3 fusion.128
  225.0 0.8 fusion.129
  225.8 1.8 copy_bitcast_fusion
  (12 shorter events, 0.2 us)
Async XLA Ops:
  7.2 98.8 %all-gather.5.cloned.1.call-start = ((), (), s32[]{:S(2)}) async-start(), calls=%async_computation | async-start | bytes 8519680 | tf_op jit(solution)/shard_map/all_gather | solution.py:31
  10.3 207.1 %all-gather.7.cloned.1.call-start = ((), (), s32[]{:S(2)}) async-start(), calls=%async_computation.1 | async-start | bytes 8519680 | tf_op jit(solution)/shard_map/all_gather | solution.py:75
  110.1 1.9 copy-start
Sparse Core Ops, SparseCore 0:
  11.9 94.0 all-gather.4
  131.2 86.2 all-gather.6
where the time goes:
time: 235 us; the launch traced here: 234 us
  waiting for transfers between devices  179 us (76%)
  blocking collectives  14.4 us (6%)
  between operations  14.2 us (6%)
  other arithmetic  10.1 us (4%)
  matrix products  9.23 us (4%)
  local copies, waits for them, and re-layouts  7.28 us (3%)
    all_gather x1, waiting for transfers between devices, shards(): pieces = lax.all_gather(own_state[None], 'ctx', axis=0, tiled=True)  93.3 us
    all_gather x1, waiting for transfers between devices, shards(): pieces = lax.all_gather(later_own[None], 'ctx', axis=0, tiled=True)  85.6 us
    psum x1, blocking collectives, shards(): lax.psum((jnp.sum(attended * attended, axis=-1), jnp.sum(scaled * attende...  14.4 us
  transfers between devices with their start and end apart: 2, of which 2 were waited for; matrix products, arithmetic and copies ran while one was open for 1% of the time, Pallas kernels for 0%

commit v1 on v0

--- a/solution.py
+++ b/solution.py
@@ -28,7 +28,9 @@
         "hte,htf->hef", key_heads, value_heads, preferred_element_type=jnp.float32
     )
     position = lax.axis_index("ctx")
-    pieces = lax.all_gather(own_state[None], "ctx", axis=0, tiled=True)
+    pieces = jnp.concatenate(
+        lax.all_to_all(jnp.stack([own_state[None]] * lax.axis_size("ctx")), "ctx", 0, 0), axis=0
+    )
     shard_index = jnp.arange(pieces.shape[0], dtype=jnp.int32)
     lower_mask = (shard_index < position).astype(jnp.float32)
     prior_state = jnp.sum(pieces * lower_mask[:, None, None, None], axis=0)

time: 235 us -> 344 us (1.46)
  waiting for transfers between devices: 179 us -> 269 us
  starting transfers between devices: 0.08 us -> 12.2 us
  blocking collectives: 14.4 us -> 19.2 us
    all_to_all x0 -> x1, waiting for transfers between devices: none -> 185 us  [shards(): lax.all_to_all(jnp.stack([own_state[None]] * lax.axis_size('ctx')), 'ctx'...]
    all_gather x1 -> x0, waiting for transfers between devices: 93.3 us -> none  [shards(): pieces = lax.all_gather(own_state[None], 'ctx', axis=0, tiled=True)]
    all_to_all x0 -> x1, starting transfers between devices: none -> 12.1 us  [shards(): lax.all_to_all(jnp.stack([own_state[None]] * lax.axis_size('ctx')), 'ctx'...]
    psum x1, blocking collectives: 14.4 us -> 19.2 us  [shards(): lax.psum((jnp.sum(attended * attended, axis=-1), jnp.sum(scaled * attende...]
    another operation x5 -> x6, local copies, waits for them, and re-layouts: 0.94 us -> 5.21 us  [the longest x1 4.27 us: shards(): jnp.stack([own_state[None]] * lax.axis_size('ctx'))]
  transfers between devices with their start and end apart: 2 -> 2, of which waited for: 2 -> 2; matrix products, arithmetic and copies ran while one was open for 1% -> 0% of each run, Pallas kernels for 0% -> 0%
where the time goes in v1:
time: 344 us; the launch traced here: 343 us
  waiting for transfers between devices  269 us (78%)
  blocking collectives  19.2 us (6%)
  between operations  14.2 us (4%)
  starting transfers between devices  12.2 us (4%)
  local copies, waits for them, and re-layouts  10.6 us (3%)
  other arithmetic  9.42 us (3%)
  matrix products  8.58 us (2%)
    all_to_all x1, waiting for transfers between devices, shards(): lax.all_to_all(jnp.stack([own_state[None]] * lax.axis_size('ctx')), 'ctx'...  185 us
    all_gather x1, waiting for transfers between devices, shards(): pieces = lax.all_gather(later_own[None], 'ctx', axis=0, tiled=True)  83.9 us
    psum x1, blocking collectives, shards(): lax.psum((jnp.sum(attended * attended, axis=-1), jnp.sum(scaled * attende...  19.2 us
    all_to_all x1, starting transfers between devices, shards(): lax.all_to_all(jnp.stack([own_state[None]] * lax.axis_size('ctx')), 'ctx'...  12.1 us
  transfers between devices with their start and end apart: 2, of which 2 were waited for; matrix products, arithmetic and copies ran while one was open for 0% of the time, Pallas kernels for 0%

profile of v1, /device:TPU:1, one launch (start us, length us, event | category | flops | bytes accessed | tf_op | source)
XLA Modules:
  0.0 343.3 jit_solution(9231405420322590191)
XLA Ops:
  7.2 1.1 copy.70
  8.3 1.1 copy.71
  9.4 0.2 fusion.82
  9.6 4.3 %stack.3 = f32[64,1,2,128,128]{4,3,2,1,0:T(8,128)} broadcast(f32[2,128,128]{2,1,0:T(8,128)S(1)} %fusion.82), dimensions={2,3,4} | broadcast | bytes 8519680 | tf_op jit(solution)/shard_map/stack | solution.py:32
  13.9 12.1 %all-to-all-start = ((f32[64,1,2,128,128]{4,3,2,1,0:T(8,128)}), f32[64,1,2,128,128]{4,3,2,1,0:T(8,128)}, u32[]{:S(2)}, u32[]{:S(2)}) async-start(f32[64,1,2,128,128]{4,3,2,1,0:T(8,128)} %stack.3), calls=%async_computation | async-start | bytes 16777216 | tf_op jit(solution)/shard_map/all_to_all | solution.py:32
  26.0 0.0 all-gather.3.cloned.1.call-start
  26.1 0.2 copy.74
  26.2 0.2 copy.75
  26.4 0.1 copy.69
  26.6 0.2 copy.73
  26.8 185.0 %all-to-all-done = f32[64,1,2,128,128]{4,3,2,1,0:T(8,128)} async-done(((f32[64,1,2,128,128]{4,3,2,1,0:T(8,128)}), f32[64,1,2,128,128]{4,3,2,1,0:T(8,128)}, u32[]{:S(2)}, u32[]{:S(2)}) %all-to-all-start) | async-done | bytes 8388640 | tf_op jit(solution)/shard_map/all_to_all | solution.py:32
  211.8 4.1 %fusion.73 = bf16[2,128,128]{2,1,0:T(8,128)(2,1)S(1)} fusion(f32[64,1,2,128,128]{4,3,2,1,0:T(8,128)} %all-to-all-done, f32[64]{0:T(128)S(1)} %compare_convert_fusion.1), kind=kLoop, calls=%fused_computation.83 | loop fusion | flops 4161536 | bytes 8454400 | tf_op jit(solution)/shard_map/reduce_sum | solution.py:36
  215.9 0.1 broadcast.24.clone
  216.0 1.6 while.41
  216.0 0.3 bitcast_dynamic-update-slice_fusion.4
  216.3 0.3 fusion.135
  216.6 0.2 fusion.136
  216.8 0.3 bitcast_dynamic-update-slice_fusion.4
  217.1 0.3 fusion.135
  217.4 0.2 fusion.136
  217.6 0.1 fusion.79
  217.8 0.1 fusion.76
  218.0 19.2 %all-reduce = (f32[512]{0:T(512)S(1)}, f32[512]{0:T(512)S(1)}) all-reduce(f32[512]{0:T(512)S(1)} %fusion.79, f32[512]{0:T(512)S(1)} %fusion.76), channel_id=1, replica_groups=mesh['ctx'=64,'tp'=8] {'tp'}, use_global_device_ids=true, to_apply=%region_4.5 | all-reduce | flops 1024 | bytes 8192 | tf_op jit(solution)/shard_map/psum | solution.py:50
  237.2 0.9 fusion.80
  238.1 0.1 broadcast.24
  238.2 3.4 while.42
  238.2 0.3 bitcast_dynamic-update-slice_fusion.5
  238.5 0.3 fusion.143
  238.9 0.2 fusion.144
  239.1 0.9 fusion.145
  239.9 0.3 bitcast_dynamic-update-slice_fusion.5
  240.2 0.3 fusion.143
  240.6 0.2 fusion.144
  240.8 0.9 fusion.145
  241.7 0.7 copy_bitcast_fusion.2
  242.4 83.9 %all-gather.3.cloned.1.call-done = f32[128,128,128]{2,1,0:T(8,128)} async-done(((f32[2,128,128]{2,1,0:T(8,128)}), f32[128,128,128]{2,1,0:T(8,128)}) %all-gather.3.cloned.1.call-update) | async-done | bytes 8388624 | tf_op jit(solution)/shard_map/all_gather | solution.py:77
  326.3 4.1 %multiply_reduce_fusion = bf16[2,128,128]{2,1,0:T(8,128)(2,1)S(1)} fusion(f32[64,2,128,128]{3,2,1,0:T(8,128)} %bitcast.216, f32[64]{0:T(128)S(1)} %compare_convert_fusion), kind=kLoop, calls=%fused_computation.84 | loop fusion | flops 4161536 | bytes 8454400 | tf_op jit(solution)/shard_map/reduce_sum | solution.py:80
  330.4 0.7 broadcast.26.clone.1
  331.2 3.5 %while.40 = (s32[]{:T(128)}, bf16[2,512,128]{2,1,0:T(8,128)(2,1)S(1)}, bf16[2,512,128]{2,1,0:T(8,128)(2,1)}, bf16[2,512,512]{2,1,0:T(8,128)(2,1)S(1)}, bf16[2,51...) while((s32[]{:T(128)}, ...), condition=%wide.region_11.12_spmd, body=%wide.region_10.11_spmd.sunk | while | flops 168034304 | bytes 2954349 | solution.py:95
  331.2 0.3 fusion.127
  331.5 0.2 fusion.128
  331.7 0.3 fusion.129
  332.1 0.8 fusion.130
  332.9 0.3 fusion.127
  333.2 0.2 fusion.128
  333.5 0.3 fusion.129
  333.8 0.8 fusion.130
  334.6 1.8 copy_bitcast_fusion
  (16 shorter events, 0.1 us)
Async XLA Ops:
  13.9 12.6 %copy-start.1 = (bf16[512,256]{1,0:T(8,128)(2,1)S(1)}, bf16[512,256]{1,0:T(8,128)(2,1)}, u32[]{:S(2)}) copy-start(bf16[512,256]{1,0:T(8,128)(2,1)} %param.11) | copy-start | bytes 786436
  13.9 12.9 %copy-start.2 = (bf16[256]{0:T(256)(128)(2,1)S(1)}, bf16[256]{0:T(256)(128)(2,1)}, u32[]{:S(2)}) copy-start(bf16[256]{0:T(256)(128)(2,1)} %param.14) | copy-start | bytes 1540
  13.9 197.9 %all-to-all-start = ((f32[64,1,2,128,128]{4,3,2,1,0:T(8,128)}), f32[64,1,2,128,128]{4,3,2,1,0:T(8,128)}, u32[]{:S(2)}, u32[]{:S(2)}) async-start(f32[64,1,2,128,128]{4,3,2,1,0:T(8,128)} %stack.3), calls=%async_computation | async-start | bytes 16777216 | tf_op jit(solution)/shard_map/all_to_all | solution.py:32
  26.0 300.3 %all-gather.3.cloned.1.call-start = ((), (), s32[]{:S(2)}) async-start(), calls=%async_computation.1 | async-start | bytes 8519680 | tf_op jit(solution)/shard_map/all_gather | solution.py:77
  215.9 1.9 copy-start
Sparse Core Ops, SparseCore 0:
  241.8 84.4 all-gather.2
